TPU v7x, 256 devices: a whole 4x4x8 slice. The times are simulated.
256 devices in a mesh: row: 16 (over y_lo, x, core), col: 16 (over y_hi, z).
Axes of the slice: x: 4, y: 4 (y_hi: 2, y_lo: 2; y = y_hi * 2 + y_lo), z: 8, core: 2. Of those that a mesh axis runs over, the one named last changes fastest.
Arguments:
- val_orb: bfloat16 [64, 2048], replicated, may hold values from -6 to 6
- con_orb: bfloat16 [512, 2048], replicated, may hold values from -6 to 6
- val_energy: float32 [64], replicated, may hold values from -1.5 to -0.5
- con_energy: float32 [512], replicated, may hold values from 0.5 to 2
- points: int32 [1024], replicated, may hold values from 0 to 2047, as said below
- val_band: int32 [1048576], P(('row', 'col')), may hold values from 0 to 63
- con_band: int32 [1048576], P(('row', 'col')), may hold values from 0 to 511
- kernel: bfloat16 [1024, 1024], replicated
- trial_vecs: bfloat16 [1048576, 128], P(('row', 'col')), may hold values from -6 to 6
Outputs:
- first_degree: bfloat16 [1048576, 128], P(('row', 'col'))
- filtered: float32 [1048576, 128], P(('row', 'col'))
Inputs may be any that keep to these rules, and one draw needn't show every extreme that they name: Distinct grid points.
All inputs are finite; a program needn't handle non-finite values.
Results may differ from a plain program's by a relative error of at most 0.0042.
Values sent between devices are 32-bit elements; how exact they have to be, the bound alone decides.
A program may use at most 128 MiB of HBM per device.

v0:
```python
import jax
import jax.numpy as jnp
from jax import lax
from jax.sharding import PartitionSpec as P

filter_center = 2.25
filter_half = 1.25


def factor_rows(val_points, con_points, val_band, con_band):
    product = jnp.take(val_points, val_band, axis=0).astype(jnp.float32) * jnp.take(
        con_points, con_band, axis=0
    ).astype(jnp.float32)
    return product.astype(jnp.bfloat16)


def shards(
    val_orb, con_orb, val_energy, con_energy, points, val_band, con_band, kernel, trial_vecs
):
    val_points = jnp.take(val_orb, points, axis=1)
    con_points = jnp.take(con_orb, points, axis=1)
    energy = (jnp.take(con_energy, con_band) - jnp.take(val_energy, val_band))[:, None]
    own_rows = factor_rows(val_points, con_points, val_band, con_band)
    kernel_wide = kernel.astype(jnp.float32)
    rows_wide = own_rows.astype(jnp.float32)

    def apply_kernel(vectors):
        partial_proj = lax.dot_general(
            own_rows, vectors, (((0,), (0,)), ((), ())), preferred_element_type=jnp.float32
        )
        projected = lax.psum(partial_proj, ("row", "col"))
        mixed = jnp.dot(kernel_wide, projected, precision=lax.Precision.HIGHEST)
        return jnp.dot(rows_wide, mixed, precision=lax.Precision.HIGHEST)

    start_vecs = trial_vecs.astype(jnp.float32)
    first = ((energy - filter_center) * start_vecs + apply_kernel(trial_vecs)) / filter_half
    first_degree = first.astype(jnp.bfloat16)
    first_wide = first_degree.astype(jnp.float32)
    filtered = (
        2.0 * ((energy - filter_center) * first_wide + apply_kernel(first_degree)) / filter_half
        - start_vecs
    )
    return (first_degree, filtered)


def solution(mesh):
    placed = (
        P(),
        P(),
        P(),
        P(),
        P(),
        P(("row", "col")),
        P(("row", "col")),
        P(),
        P(("row", "col"), None),
    )
    return jax.shard_map(
        shards,
        mesh=mesh,
        in_specs=placed,
        out_specs=(P(("row", "col"), None), P(("row", "col"), None)),
        check_vma=False,
    )
```

profile of v0, /device:TPU:1, one launch (start us, length us, event | category | flops | bytes accessed | tf_op | source)
XLA Modules:
  0.0 708.7 jit_solution(5484198504451303308)
XLA Ops:
  7.2 0.0 copy-start
  7.2 0.0 all-reduce.3.cloned.1.call-start
  7.2 0.8 fusion.8
  8.1 0.7 compare_and_fusion.2
  8.8 0.0 copy-start.11
  8.8 1.6 fusion.12
  10.3 2.1 fusion.9
  12.4 2.1 fusion.10
  14.5 2.1 fusion.11
  16.6 1.3 fusion.7
  17.9 1.3 compare_and_fusion
  19.2 0.0 copy-start.8
  19.2 0.0 copy-start.5
  19.2 4.0 copy.17
  23.2 5.8 gather_fusion.3
  29.0 1.2 select_bitcast_fusion
  30.2 1.5 copy.18
  31.7 0.0 copy-done.11
  31.7 0.0 copy-done.8
  31.7 0.0 copy-done.5
  31.8 1.0 copy.15
  32.8 5.2 gather_fusion.1
  38.0 1.2 select_bitcast_fusion.1
  39.1 0.1 copy.16
  39.2 0.0 copy-start.1
  39.3 18.3 %gather_fusion.4 = bf16[4096,1024]{1,0:T(8,128)(2,1)} fusion(bf16[512,1024]{1,0:T(8,128)(2,1)S(1)} %copy.18, s32[4096]{0:T(1024)S(1)} %fusion.6), kind=kCustom, calls=%fused_computation.4 | custom fusion | bytes 16793600 | tf_op jit(solution)/shard_map/jit(_take)/gather | solution.py:11
  57.5 0.0 copy-done.1
  57.5 0.0 copy-start.7
  57.5 25.9 %gather_fusion = f32[4096]{0:T(1024)S(1)} fusion(f32[512]{0:T(512)S(1)} %copy-done.1, s32[4096]{0:T(1024)S(1)} %fusion.6), kind=kCustom, calls=%fused_computation | custom fusion | bytes 49152 | tf_op jit(solution)/shard_map/jit(_take)/gather | solution.py:22
  83.4 0.0 copy-done.7
  83.4 0.0 copy-start.6
  83.4 0.0 copy-start.9
  83.4 0.0 copy-start.10
  83.5 18.3 %gather_fusion.2 = bf16[4096,1024]{1,0:T(8,128)(2,1)} fusion(bf16[64,1024]{1,0:T(8,128)(2,1)S(1)} %copy.16, s32[4096]{0:T(1024)S(1)} %copy-done.7), kind=kCustom, calls=%fused_computation.2 | custom fusion | bytes 16793600 | tf_op jit(solution)/shard_map/jit(_take)/gather | solution.py:11
  101.7 0.0 copy-done.6
  101.7 0.0 copy-done.9
  101.7 40.1 %fusion.5 = (f32[4096]{0:T(1024)S(1)}, pred[4096]{0:T(1024)(128)(4,1)S(1)}) fusion(f32[4096]{0:T(1024)S(1)} %gather_fusion, s32[4096]{0:T(1024)S(1)} %copy-done.6, f32[]{:T(128)} %bitcast, f32[]{:T(128)} %bitcast.1, f32[]{:T(128)} %bitcast.2, f32[]{:T(128)} %bitcast.3, f32[]{:T(128)} %bitcast.4, f32[]{:T(128)} %bitcast.5, f32[]{:T(128)} %bitcast.6, ...), kind=kLoop, calls=%fused_computation.19 | loop fusion | flops 581632 | bytes 69888 | tf_op jit(solution)/shard_map/sub | solution.py:36
  141.8 0.0 copy-done.10
  141.8 0.0 copy-start.3
  141.8 7.7 %multiply_convert_fusion = bf16[4096,1024]{1,0:T(8,128)(2,1)S(1)} fusion(bf16[4096,1024]{1,0:T(8,128)(2,1)} %gather_fusion.4, bf16[4096,1024]{1,0:T(8,128)(2,1)} %gather_fusion.2, pred[4096]{0:T(1024)(128)(4,1)S(1)} %get-tuple-element.3, pred[4096]{0:T(1024)(128)(4,1)S(1)} %copy-done.10), kind=kLoop, calls=%fused_computation.5 | loop fusion | flops 25165824 | bytes 25174016 | tf_op jit(solution)/shard_map/convert_element_type | solution.py:14
  149.5 0.0 copy-start.2
  149.5 3.2 copy-done.2
  152.8 0.0 copy-done.3
  152.8 3.1 fusion.13
  155.9 0.0 all-reduce.3.cloned.1.call-update
  155.9 0.0 all-reduce.5.cloned.1.call-start
  156.0 257.9 %all-reduce.3.cloned.1.call-done = f32[1024,128]{1,0:T(8,128)} async-done(((f32[1024,128]{1,0:T(8,128)}), f32[1024,128]{1,0:T(8,128)}) %all-reduce.3.cloned.1.call-update) | async-done | bytes 524304 | tf_op jit(solution)/shard_map/psum | solution.py:31
  413.9 0.0 copy-done
  413.9 3.3 fusion.14
  417.2 9.3 %fusion.3 = bf16[4096,128]{1,0:T(8,128)(2,1)S(1)} fusion(bf16[4096,1024]{1,0:T(8,128)(2,1)} %copy-done.2, f32[128,1024]{1,0:T(8,128)S(1)} %fusion.14, bf16[4096,128]{1,0:T(8,128)(2,1)S(1)} %copy-done.3, f32[4096]{0:T(1024)S(1)} %get-tuple-element.2), kind=kOutput, calls=%fused_computation.11 | convolution fusion | flops 6445072384 | bytes 11026432 | tf_op jit(solution)/shard_map/dot_general | solution.py:33
  426.5 0.0 copy-start.4
  426.5 1.0 copy-done.4
  427.5 6.6 fusion.15
  434.1 0.0 all-reduce.5.cloned.1.call-update
  434.1 254.2 %all-reduce.5.cloned.1.call-done = f32[1024,128]{1,0:T(8,128)} async-done(((f32[1024,128]{1,0:T(8,128)}), f32[1024,128]{1,0:T(8,128)}) %all-reduce.5.cloned.1.call-update) | async-done | bytes 524304 | tf_op jit(solution)/shard_map/psum | solution.py:31
  688.3 3.3 fusion.16
  691.6 10.2 %fusion.1 = f32[4096,128]{1,0:T(8,128)} fusion(bf16[4096,1024]{1,0:T(8,128)(2,1)} %copy-done.2, f32[128,1024]{1,0:T(8,128)S(1)} %fusion.16, bf16[4096,128]{1,0:T(8,128)(2,1)S(1)} %copy-done.3, bf16[4096,128]{1,0:T(8,128)(2,1)} %copy-done.4, f32[4096]{0:T(1024)S(1)} %get-tuple-element.2), kind=kOutput, calls=%fused_computation.8 | convolution fusion | flops 6445596672 | bytes 13123584 | tf_op jit(solution)/shard_map/dot_general | solution.py:33
  (1 shorter events, 0.0 us)
Async XLA Ops:
  7.2 406.7 %copy-start = (bf16[1024,1024]{1,0:T(8,128)(2,1)S(1)}, bf16[1024,1024]{1,0:T(8,128)(2,1)}, u32[]{:S(2)}) copy-start(bf16[1024,1024]{1,0:T(8,128)(2,1)} %param.16) | copy-start | bytes 6291460
  7.2 406.7 %all-reduce.3.cloned.1.call-start = ((), (), s32[]{:S(2)}) async-start(), calls=%async_computation | async-start | bytes 1048576 | tf_op jit(solution)/shard_map/psum | solution.py:31
  8.8 23.0 %copy-start.11 = (pred[1024]{0:T(1024)(128)(4,1)}, pred[1024]{0:T(1024)(128)(4,1)S(1)}, u32[]{:S(2)}) copy-start(pred[1024]{0:T(1024)(128)(4,1)S(1)} %compare_and_fusion.2) | copy-start | bytes 3076
  19.2 12.5 %copy-start.8 = (s32[4096]{0:T(1024)S(1)}, s32[4096]{0:T(1024)}, u32[]{:S(2)}) copy-start(s32[4096]{0:T(1024)} %param.15) | copy-start | bytes 49156
  19.2 12.5 %copy-start.5 = (bf16[64,2048]{1,0:T(8,128)(2,1)S(1)}, bf16[64,2048]{1,0:T(8,128)(2,1)}, u32[]{:S(2)}) copy-start(bf16[64,2048]{1,0:T(8,128)(2,1)} %param.9) | copy-start | bytes 786436
  39.2 18.3 %copy-start.1 = (f32[512]{0:T(512)S(1)}, f32[512]{0:T(512)}, u32[]{:S(2)}) copy-start(f32[512]{0:T(512)} %param.12) | copy-start | bytes 6148
  57.5 25.9 %copy-start.7 = (s32[4096]{0:T(1024)S(1)}, s32[4096]{0:T(1024)}, u32[]{:S(2)}) copy-start(s32[4096]{0:T(1024)} %fusion.7) | copy-start | bytes 49156
  83.4 18.3 %copy-start.6 = (s32[4096]{0:T(1024)S(1)}, s32[4096]{0:T(1024)}, u32[]{:S(2)}) copy-start(s32[4096]{0:T(1024)} %param.14) | copy-start | bytes 49156
  83.4 18.3 %copy-start.9 = (s32[4096]{0:T(1024)S(1)}, s32[4096]{0:T(1024)}, u32[]{:S(2)}) copy-start(s32[4096]{0:T(1024)} %param.15) | copy-start | bytes 49156
  83.4 58.3 %copy-start.10 = (pred[4096]{0:T(1024)(128)(4,1)S(1)}, pred[4096]{0:T(1024)(128)(4,1)}, u32[]{:S(2)}) copy-start(pred[4096]{0:T(1024)(128)(4,1)} %compare_and_fusion) | copy-start | bytes 12292
  141.8 11.0 %copy-start.3 = (bf16[4096,128]{1,0:T(8,128)(2,1)S(1)}, bf16[4096,128]{1,0:T(8,128)(2,1)}, u32[]{:S(2)}) copy-start(bf16[4096,128]{1,0:T(8,128)(2,1)} %param.17) | copy-start | bytes 3145732
  149.5 3.2 copy-start.2
  155.9 532.4 %all-reduce.5.cloned.1.call-start = ((), (), s32[]{:S(2)}) async-start(), calls=%async_computation.1 | async-start | bytes 1048576 | tf_op jit(solution)/shard_map/psum | solution.py:31
  426.5 1.0 copy-start.4
Sparse Core Ops, SparseCore 0:
  156.1 257.7 all-reduce.2
  434.2 254.0 all-reduce.4
where the time goes:
time: 711 us; the launch traced here: 709 us
  waiting for transfers between devices  512 us (72%)
  local copies, waits for them, and re-layouts  92.1 us (13%)
  other arithmetic  54.3 us (8%)
  matrix products  35.8 us (5%)
  between operations  14.2 us (2%)
    psum x2, waiting for transfers between devices, apply_kernel(): projected = lax.psum(partial_proj, ('row', 'col'))  512 us
    sub x1, other arithmetic, shards(): energy - filter_center  40.1 us
    gather x1, local copies, waits for them, and re-layouts, shards(): jnp.take(con_energy, con_band) - jnp.take(val_energy, val_band)  25.9 us
    dot_general x2, matrix products, apply_kernel(): return jnp.dot(rows_wide, mixed, precision=lax.Precision.HIGHEST)  19.5 us
    gather x1, local copies, waits for them, and re-layouts, factor_rows(): jnp.take(con_points, con_band, axis=0).astype(jnp.float32)  18.3 us
    gather x1, local copies, waits for them, and re-layouts, factor_rows(): jnp.take(val_points, val_band, axis=0).astype(jnp.float32)  18.3 us
  transfers between devices with their start and end apart: 2, of which 2 were waited for; matrix products, arithmetic and copies ran while one was open for 0% of the time, Pallas kernels for 0%

commit v1 on v0

v1 whole, which is shorter than its diff:
```python
import jax
import jax.numpy as jnp
from jax import lax
from jax.experimental import pallas as pl
from jax.experimental.pallas import tpu as pltpu
from jax.sharding import PartitionSpec as P

filter_center = 2.25
filter_half = 1.25

F32 = jnp.float32
BF16 = jnp.bfloat16
MESH = pl.DeviceIdType.MESH

NMU, NVEC, NV, NC, NGRID = 1024, 128, 64, 512, 2048
PAIRS = 4096
NB = 4
MB = NMU // NB
PC = 512
NPC = PAIRS // PC

CORE, PLANE, DEPTH, GATHER, JOIN = range(5)
PLANE_STEPS = sorted(
    range(1, 16), key=lambda d: -(min(d // 4, 4 - d // 4) + min(d % 4, 4 - d % 4))
)
DEPTH_STEPS = sorted(range(1, 8), key=lambda d: -min(d, 8 - d))


def dot(a, b):
    return jnp.dot(a, b, preferred_element_type=F32)


def dot_tn(a, b):
    return lax.dot_general(a, b, (((0,), (0,)), ((), ())), preferred_element_type=F32)


def halves(wide):
    high = wide.astype(BF16)
    low = (wide - high.astype(F32)).astype(BF16)
    return high, low


class Place:
    def __init__(self):
        row, col = lax.axis_index("row"), lax.axis_index("col")
        self.core = lax.rem(row, 2)
        self.x = lax.rem(lax.div(row, 2), 4)
        self.y = lax.div(col, 8) * 2 + lax.div(row, 8)
        self.z = lax.rem(col, 8)

    def at(self, x, y, z, core):
        row = (lax.rem(y, 2) * 4 + x) * 2 + core
        col = lax.div(y, 2) * 8 + z
        return (row, col)

    def partner(self):
        return self.at(self.x, self.y, self.z, 1 - self.core)

    def plane(self, d):
        x = lax.rem(self.x + d % 4, 4)
        y = lax.rem(self.y + d // 4, 4)
        return self.at(x, y, self.z, self.core)

    def depth(self, d):
        return self.at(self.x, self.y, lax.rem(self.z + d, 8), self.core)

    def everyone(self):
        return (
            [self.partner()]
            + [self.plane(d) for d in PLANE_STEPS]
            + [self.depth(d) for d in DEPTH_STEPS]
        )


class Sum:
    def __init__(self, place, part, core_in, half, plane_in, depth_in, whole, send, recv):
        self.p = place
        self.part, self.core_in, self.half = part, core_in, half
        self.plane_in, self.depth_in, self.whole = plane_in, depth_in, whole
        self.send, self.recv = send, recv
        self.slot = place.y * 4 + place.x
        self.owner = place.core * 16 + self.slot

    def copy(self, src, dst, stage, b, device):
        pltpu.make_async_remote_copy(
            src_ref=src,
            dst_ref=dst,
            send_sem=self.send.at[stage],
            recv_sem=self.recv.at[stage, b],
            device_id=device,
            device_id_type=MESH,
        ).start()

    def arrived(self, ref, stage, b):
        pltpu.make_async_copy(ref, ref, self.recv.at[stage, b]).wait()

    def sent(self, ref, stage):
        pltpu.make_async_copy(ref, ref, self.send.at[stage]).wait()

    def to_core(self, b):
        other = pl.multiple_of((1 - self.p.core) * 128, 128)
        self.copy(self.part.at[b, pl.ds(other, 128)], self.core_in.at[b], CORE, b, self.p.partner())

    def to_plane(self, b):
        self.arrived(self.core_in.at[b], CORE, b)
        own = pl.multiple_of(self.p.core * 128, 128)
        both = self.part[b, pl.ds(own, 128), :] + self.core_in[b]
        self.half[b] = both.reshape(16, 8, NVEC)
        for d in PLANE_STEPS:
            x = lax.rem(self.p.x + d % 4, 4)
            y = lax.rem(self.p.y + d // 4, 4)
            self.copy(self.half.at[b, y * 4 + x], self.plane_in.at[b, d], PLANE, b, self.p.plane(d))

    def to_depth(self, b):
        self.arrived(self.plane_in.at[b, pl.ds(1, 15)], PLANE, b)
        total = self.half[b, self.slot]
        for d in range(1, 16):
            total = total + self.plane_in[b, d]
        self.depth_in[b, 0] = total
        for d in DEPTH_STEPS:
            self.copy(self.depth_in.at[b, 0], self.depth_in.at[b, d], DEPTH, b, self.p.depth(d))

    def to_gather(self, b):
        self.arrived(self.depth_in.at[b, pl.ds(1, 7)], DEPTH, b)
        total = self.depth_in[b, 0]
        for d in range(1, 8):
            total = total + self.depth_in[b, d]
        self.whole[b, self.owner] = total
        for d in PLANE_STEPS:
            piece = self.whole.at[b, self.owner]
            self.copy(piece, piece, GATHER, b, self.p.plane(d))

    def to_join(self, b):
        self.arrived(self.plane_in.at[b, pl.ds(1, 15)], GATHER, b)
        piece = self.whole.at[b, pl.ds(self.p.core * 16, 16)]
        self.copy(piece, piece, JOIN, b, self.p.partner())

    def done(self, b):
        self.arrived(self.whole.at[b, pl.ds(0, 16)], JOIN, b)

    def close(self):
        self.sent(self.core_in, CORE)
        self.sent(self.plane_in.at[:, pl.ds(1, 15)], PLANE)
        self.sent(self.depth_in.at[:, pl.ds(1, 7)], DEPTH)
        self.sent(self.plane_in.at[:, pl.ds(1, 15)], GATHER)
        self.sent(self.whole.at[:, pl.ds(0, 16)], JOIN)


def filter_kernel(
    val_hbm, con_hbm, val_energy, con_energy, points, val_band, con_band, kernel_hbm, trial_hbm,
    first_out, filtered_out,
    orb, con_hot, val_hot, grid_hot, points_rows, rows, trial, mix, shifted, mixed_pair,
    part1, core1, half1, plane1, depth1, whole1,
    part2, core2, half2, plane2, depth2, whole2,
    load_sem, send1, recv1, send2, recv2,
):
    place = Place()
    barrier = pltpu.get_barrier_semaphore()
    for device in place.everyone():
        pl.semaphore_signal(barrier, inc=1, device_id=device, device_id_type=MESH)

    con_load = pltpu.make_async_copy(con_hbm, orb.at[pl.ds(0, NC)], load_sem.at[0])
    val_load = pltpu.make_async_copy(val_hbm, orb.at[pl.ds(NC, NV)], load_sem.at[1])
    trial_load = pltpu.make_async_copy(trial_hbm, trial, load_sem.at[2])
    mix_load = pltpu.make_async_copy(kernel_hbm, mix, load_sem.at[3])
    for load in (con_load, val_load, trial_load, mix_load):
        load.start()

    def build_hot(j, carry):
        lanes = pl.ds(pl.multiple_of(j * 128, 128), 128)
        con_row = con_band[pl.ds(j, 1), :]
        val_row = val_band[pl.ds(j, 1), :]
        for t in range(NC // 128):
            ids = lax.broadcasted_iota(jnp.int32, (128, 128), 0) + t * 128
            con_hot[t * 128 : (t + 1) * 128, lanes] = jnp.where(ids == con_row, 1.0, 0.0).astype(BF16)
        ids = lax.broadcasted_iota(jnp.int32, (NV, 128), 0)
        val_hot[:, lanes] = jnp.where(ids == val_row, 1.0, 0.0).astype(BF16)
        return carry

    lax.fori_loop(0, PAIRS // 128, build_hot, 0)
    con_load.wait()
    val_load.wait()

    sum1 = Sum(place, part1, core1, half1, plane1, depth1, whole1, send1, recv1)
    sum2 = Sum(place, part2, core2, half2, plane2, depth2, whole2, send2, recv2)

    for b in range(NB):
        for j in range(MB // 128):
            row = points[b * (MB // 128) + j : b * (MB // 128) + j + 1, :]
            for t in range(NGRID // 128):
                ids = lax.broadcasted_iota(jnp.int32, (128, 128), 0) + t * 128
                grid_hot[t * 128 : (t + 1) * 128, j * 128 : (j + 1) * 128] = jnp.where(
                    ids == row, 1.0, 0.0
                ).astype(BF16)
        points_rows[...] = dot(orb[...], grid_hot[...]).astype(BF16)

        def make_rows(j, carry):
            cols = pl.ds(pl.multiple_of(j * PC, PC), PC)
            con_part = dot_tn(points_rows[:NC, :], con_hot[:, cols])
            val_part = dot_tn(points_rows[NC:, :], val_hot[:, cols])
            rows[b * MB : (b + 1) * MB, cols] = (con_part * val_part).astype(BF16)
            return carry

        lax.fori_loop(0, NPC, make_rows, 0)
        if b == 0:
            trial_load.wait()
        part1[b] = dot(rows[b * MB : (b + 1) * MB, :], trial[...])
        if b == 0:
            pl.semaphore_wait(barrier, 23)
        sum1.to_core(b)
        if b >= 1:
            sum1.to_plane(b - 1)
        if b >= 2:
            sum1.to_depth(b - 2)
        if b >= 3:
            sum1.to_gather(b - 3)

    sum1.to_plane(NB - 1)

    con_col = jnp.broadcast_to(con_energy[...], (128, NC)).T
    val_col = jnp.broadcast_to(val_energy[...], (128, NV)).T
    con_pair = jnp.concatenate(halves(con_col), axis=1)
    val_pair = jnp.concatenate(halves(-val_col), axis=1)

    def make_shifted(j, carry):
        cols = pl.ds(pl.multiple_of(j * PC, PC), PC)
        both = dot_tn(con_hot[:, cols], con_pair) + dot_tn(val_hot[:, cols], val_pair)
        shifted[cols, :] = (both[:, :NVEC] + both[:, NVEC:]) - filter_center
        return carry

    lax.fori_loop(0, NPC, make_shifted, 0)
    mix_load.wait()

    def drain(total, plane_from, gather_from):
        for b in range(plane_from, NB):
            total.to_depth(b)
        for b in range(gather_from, NB):
            total.to_gather(b)
        for b in range(NB):
            total.to_join(b)

    def mixed_of(total):
        for b in range(NB):
            total.done(b)
            high, low = halves(total.whole[b].reshape(MB, NVEC))
            mixed_pair[b * MB : (b + 1) * MB, :NVEC] = high
            mixed_pair[b * MB : (b + 1) * MB, NVEC:] = low
        both = dot(mix[...], mixed_pair[...])
        high, low = halves(both[:, :NVEC] + both[:, NVEC:])
        mixed_pair[:, :NVEC] = high
        mixed_pair[:, NVEC:] = low

    def expand(cols):
        both = dot_tn(rows[:, cols], mixed_pair[...])
        return both[:, :NVEC] + both[:, NVEC:]

    drain(sum1, NB - 2, NB - 3)
    mixed_of(sum1)

    def first_step(j, carry):
        cols = pl.ds(pl.multiple_of(j * PC, PC), PC)
        value = shifted[cols, :] * trial[cols, :].astype(F32) + expand(cols)
        first_out[cols, :] = (value * (1.0 / filter_half)).astype(BF16)
        return carry

    lax.fori_loop(0, NPC, first_step, 0)

    for b in range(NB):
        part2[b] = dot(rows[b * MB : (b + 1) * MB, :], first_out[...])
        sum2.to_core(b)
        if b >= 1:
            sum2.to_plane(b - 1)
    sum2.to_plane(NB - 1)
    drain(sum2, 0, 0)
    mixed_of(sum2)

    def second_step(j, carry):
        cols = pl.ds(pl.multiple_of(j * PC, PC), PC)
        value = shifted[cols, :] * first_out[cols, :].astype(F32) + expand(cols)
        filtered_out[cols, :] = value * (2.0 / filter_half) - trial[cols, :].astype(F32)
        return carry

    lax.fori_loop(0, NPC, second_step, 0)
    sum1.close()
    sum2.close()


def shards(
    val_orb, con_orb, val_energy, con_energy, points, val_band, con_band, kernel, trial_vecs
):
    vmem = pl.BlockSpec(memory_space=pltpu.VMEM)
    away = pl.BlockSpec(memory_space=pl.ANY)

    def sum_buffers():
        return [
            pltpu.VMEM((NB, MB, NVEC), F32),
            pltpu.VMEM((NB, 128, NVEC), F32),
            pltpu.VMEM((NB, 16, 8, NVEC), F32),
            pltpu.VMEM((NB, 16, 8, NVEC), F32),
            pltpu.VMEM((NB, 8, 8, NVEC), F32),
            pltpu.VMEM((NB, 32, 8, NVEC), F32),
        ]

    return pl.pallas_call(
        filter_kernel,
        out_shape=(
            jax.ShapeDtypeStruct((PAIRS, NVEC), BF16),
            jax.ShapeDtypeStruct((PAIRS, NVEC), F32),
        ),
        in_specs=[away, away, vmem, vmem, vmem, vmem, vmem, away, away],
        out_specs=(vmem, vmem),
        scratch_shapes=[
            pltpu.VMEM((NC + NV, NGRID), BF16),
            pltpu.VMEM((NC, PAIRS), BF16),
            pltpu.VMEM((NV, PAIRS), BF16),
            pltpu.VMEM((NGRID, MB), BF16),
            pltpu.VMEM((NC + NV, MB), BF16),
            pltpu.VMEM((NMU, PAIRS), BF16),
            pltpu.VMEM((PAIRS, NVEC), BF16),
            pltpu.VMEM((NMU, NMU), BF16),
            pltpu.VMEM((PAIRS, NVEC), F32),
            pltpu.VMEM((NMU, 2 * NVEC), BF16),
        ]
        + sum_buffers()
        + sum_buffers()
        + [
            pltpu.SemaphoreType.DMA((4,)),
            pltpu.SemaphoreType.DMA((5,)),
            pltpu.SemaphoreType.DMA((5, NB)),
            pltpu.SemaphoreType.DMA((5,)),
            pltpu.SemaphoreType.DMA((5, NB)),
        ],
        compiler_params=pltpu.CompilerParams(
            collective_id=0, has_side_effects=True, vmem_limit_bytes=48 * 1024 * 1024
        ),
    )(
        val_orb,
        con_orb,
        val_energy.reshape(1, NV),
        con_energy.reshape(1, NC),
        points.reshape(8, 128),
        val_band.reshape(PAIRS // 128, 128),
        con_band.reshape(PAIRS // 128, 128),
        kernel,
        trial_vecs,
    )


def solution(mesh):
    placed = (P(), P(), P(), P(), P(), P(("row", "col")), P(("row", "col")), P(), P(("row", "col"), None))
    return jax.shard_map(
        shards,
        mesh=mesh,
        in_specs=placed,
        out_specs=(P(("row", "col"), None), P(("row", "col"), None)),
        check_vma=False,
    )
```

time: 711 us -> 82 us (0.12)
  waiting for transfers between devices: 512 us -> 0 us
  local copies, waits for them, and re-layouts: 92.1 us -> 7.91 us
  Pallas kernels: 0 us -> 73.1 us
  other arithmetic: 54.3 us -> 0 us
  matrix products: 35.8 us -> 0 us
  between operations: 14.2 us -> 0.66 us
    psum x2 -> x0, waiting for transfers between devices: 512 us -> none  [apply_kernel(): projected = lax.psum(partial_proj, ('row', 'col'))]
    gather x9 -> x0, local copies, waits for them, and re-layouts: 81.3 us -> none  [the longest x1 25.9 us: shards(): jnp.take(con_energy, con_band) - jnp.take(val_energy, val_band)]
    pallas_call x0 -> x1, Pallas kernels: none -> 73.1 us  [shards(): pl.pallas_call(filter_kernel, out_shape=(jax.ShapeDtypeStruct((PAIRS, NVE...]
    sub x1 -> x0, other arithmetic: 40.1 us -> none  [shards(): energy - filter_center]
    dot_general x6 -> x0, matrix products: 35.8 us -> none  [the longest x2 19.5 us: apply_kernel(): return jnp.dot(rows_wide, mixed, precision=lax.Precision.HIGHEST)]
    convert_element_type x1 -> x0, other arithmetic: 7.71 us -> none  [factor_rows(): return product.astype(jnp.bfloat16)]
  transfers between devices with their start and end apart: 2 -> 0, of which waited for: 2 -> 0; matrix products, arithmetic and copies ran while one was open for 0% -> 0% of each run, Pallas kernels for 0% -> 0%
where the time goes in v1:
time: 82 us; the launch traced here: 81.7 us
  Pallas kernels  73.1 us (89%)
  local copies, waits for them, and re-layouts  7.91 us (10%)
    pallas_call x1, Pallas kernels, shards(): pl.pallas_call(filter_kernel, out_shape=(jax.ShapeDtypeStruct((PAIRS, NVE...  73.1 us
    unnamed x16, local copies, waits for them, and re-layouts  7.91 us

profile of v1, /device:TPU:1, one launch (start us, length us, event | category | flops | bytes accessed | tf_op | source)
XLA Modules:
  0.0 81.7 jit_solution(3686424041197426534)
XLA Ops:
  0.6 0.0 copy-start
  0.6 1.2 %copy-done = bf16[4096,128]{1,0:T(8,128)(2,1)S(1)} copy-done((bf16[4096,128]{1,0:T(8,128)(2,1)S(1)}, bf16[4096,128]{1,0:T(8,128)(2,1)}, u32[]{:S(2)}) %copy-start) | copy-done | bytes 1048600
  1.9 0.0 copy-start.1
  1.9 0.9 %copy-done.1 = bf16[64,2048]{1,0:T(8,128)(2,1)S(1)} copy-done((bf16[64,2048]{1,0:T(8,128)(2,1)S(1)}, bf16[64,2048]{1,0:T(8,128)(2,1)}, u32[]{:S(2)}) %copy-start.1) | copy-done | bytes 262168
  2.8 0.0 copy-start.2
  2.8 0.7 copy-done.2
  3.5 0.0 copy-start.3
  3.5 0.7 copy-done.3
  4.2 0.0 copy-start.4
  4.2 0.7 copy-done.4
  4.9 0.0 copy-start.5
  4.9 0.7 copy-done.5
  5.6 0.0 copy-start.6
  5.6 0.7 copy-done.6
  6.3 73.1 %shard_map.104 = (bf16[4096,128]{1,0:T(8,128)(2,1)S(1)}, f32[4096,128]{1,0:T(8,128)S(1)}) custom-call(bf16[64,2048]{1,0:T(8,128)(2,1)S(1)} %copy-done.1, bf16[512,2048]{1,0:T(8,128)(2,1)} %con_hbm.1, f32[1,64]{1,0:T(1,128)S(1)} %bitcast.9, f32[1,512]{1,0:T(1,128)S(1)} %bitcast.8, s32[8,128]{1,0:T(8,128)S(1)} %bitcast.7, s32[32,128]{1,0:T(8,128)S(1)} %bitcast.5, ...), custom_call_target="tpu_custom_call" | custom-call | tf_op jit(solution)/shard_map/pallas_call | solution.py:304
  79.4 1.0 %copy.13 = bf16[4096,128]{1,0:T(8,128)(2,1)} copy(bf16[4096,128]{1,0:T(8,128)(2,1)S(1)} %get-tuple-element.4) | data formatting | bytes 2097152
  80.3 1.3 %copy.14 = f32[4096,128]{1,0:T(8,128)} copy(f32[4096,128]{1,0:T(8,128)S(1)} %get-tuple-element.5) | data formatting | bytes 4194304
Async XLA Ops:
  0.6 1.2 %copy-start = (bf16[4096,128]{1,0:T(8,128)(2,1)S(1)}, bf16[4096,128]{1,0:T(8,128)(2,1)}, u32[]{:S(2)}) copy-start(bf16[4096,128]{1,0:T(8,128)(2,1)} %trial_hbm.1) | copy-start | bytes 3145732
  1.9 0.9 %copy-start.1 = (bf16[64,2048]{1,0:T(8,128)(2,1)S(1)}, bf16[64,2048]{1,0:T(8,128)(2,1)}, u32[]{:S(2)}) copy-start(bf16[64,2048]{1,0:T(8,128)(2,1)} %val_hbm.1) | copy-start | bytes 786436
  2.8 0.7 copy-start.2
  3.5 0.7 copy-start.3
  4.2 0.7 copy-start.4
  4.9 0.7 copy-start.5
  5.6 0.7 copy-start.6

commit v2 on v1

--- a/solution.py
+++ b/solution.py
@@ -28,10 +28,6 @@
 
 def dot(a, b):
     return jnp.dot(a, b, preferred_element_type=F32)
-
-
-def dot_tn(a, b):
-    return lax.dot_general(a, b, (((0,), (0,)), ((), ())), preferred_element_type=F32)
 
 
 def halves(wide):
@@ -147,64 +143,92 @@
 
 
 def filter_kernel(
-    val_hbm, con_hbm, val_energy, con_energy, points, val_band, con_band, kernel_hbm, trial_hbm,
+    val_hbm, con_hbm, val_energy_hbm, con_energy_hbm, points_hbm, val_band_hbm, con_band_hbm,
+    kernel_hbm, trial_hbm,
     first_out, filtered_out,
-    orb, con_hot, val_hot, grid_hot, points_rows, rows, trial, mix, shifted, mixed_pair,
+    val_energy, con_energy, points, val_band, con_band,
+    orb, con_hot, val_hot, grid_hot, points_rows, rows, trial, turned, mix, shifted, mixed_pair,
     part1, core1, half1, plane1, depth1, whole1,
     part2, core2, half2, plane2, depth2, whole2,
     load_sem, send1, recv1, send2, recv2,
 ):
+    def load(src, dst, k):
+        copy = pltpu.make_async_copy(src, dst, load_sem.at[k])
+        copy.start()
+        return copy
+
+    points_load = load(points_hbm, points, 0)
+    con_band_load = load(con_band_hbm, con_band, 1)
+    val_band_load = load(val_band_hbm, val_band, 2)
+    con_load = load(con_hbm, orb.at[pl.ds(0, NC)], 3)
+    val_load = load(val_hbm, orb.at[pl.ds(NC, NV)], 4)
+    trial_load = load(trial_hbm, trial, 5)
+    con_energy_load = load(con_energy_hbm, con_energy, 6)
+    val_energy_load = load(val_energy_hbm, val_energy, 7)
+    mix_load = load(kernel_hbm, mix, 8)
+
     place = Place()
     barrier = pltpu.get_barrier_semaphore()
     for device in place.everyone():
         pl.semaphore_signal(barrier, inc=1, device_id=device, device_id_type=MESH)
 
-    con_load = pltpu.make_async_copy(con_hbm, orb.at[pl.ds(0, NC)], load_sem.at[0])
-    val_load = pltpu.make_async_copy(val_hbm, orb.at[pl.ds(NC, NV)], load_sem.at[1])
-    trial_load = pltpu.make_async_copy(trial_hbm, trial, load_sem.at[2])
-    mix_load = pltpu.make_async_copy(kernel_hbm, mix, load_sem.at[3])
-    for load in (con_load, val_load, trial_load, mix_load):
-        load.start()
+    def build_grid(b, t):
+        ids = lax.broadcasted_iota(jnp.int32, (128, 128), 0) + t * 128
+        for j in range(MB // 128):
+            k = b * (MB // 128) + j
+            grid_hot[b % 2, pl.ds(pl.multiple_of(t * 128, 128), 128), j * 128 : (j + 1) * 128] = jnp.where(
+                ids == points[k : k + 1, :], 1.0, 0.0
+            ).astype(BF16)
+
+    points_load.wait()
+    for t in range(NGRID // 128):
+        build_grid(0, t)
+    con_band_load.wait()
+    val_band_load.wait()
 
     def build_hot(j, carry):
-        lanes = pl.ds(pl.multiple_of(j * 128, 128), 128)
-        con_row = con_band[pl.ds(j, 1), :]
-        val_row = val_band[pl.ds(j, 1), :]
+        both = (con_band[pl.ds(j, 1), :] * NV + val_band[pl.ds(j, 1), :]).astype(F32)
+        column = jnp.broadcast_to(both, (128, 128)).T.astype(jnp.int32)
+        con_column = lax.shift_right_logical(column, 6)
+        val_column = lax.bitwise_and(column, NV - 1)
+        ids = lax.broadcasted_iota(jnp.int32, (128, 128), 1)
+        pairs = pl.ds(pl.multiple_of(j * 128, 128), 128)
         for t in range(NC // 128):
-            ids = lax.broadcasted_iota(jnp.int32, (128, 128), 0) + t * 128
-            con_hot[t * 128 : (t + 1) * 128, lanes] = jnp.where(ids == con_row, 1.0, 0.0).astype(BF16)
-        ids = lax.broadcasted_iota(jnp.int32, (NV, 128), 0)
-        val_hot[:, lanes] = jnp.where(ids == val_row, 1.0, 0.0).astype(BF16)
+            con_hot[pairs, t * 128 : (t + 1) * 128] = jnp.where(ids + t * 128 == con_column, 1.0, 0.0).astype(BF16)
+        val_hot[pairs, :] = jnp.where(ids == val_column, 1.0, 0.0).astype(BF16)
         return carry
 
     lax.fori_loop(0, PAIRS // 128, build_hot, 0)
     con_load.wait()
     val_load.wait()
+    trial_load.wait()
 
     sum1 = Sum(place, part1, core1, half1, plane1, depth1, whole1, send1, recv1)
     sum2 = Sum(place, part2, core2, half2, plane2, depth2, whole2, send2, recv2)
 
+    def project(total, b):
+        both = dot(turned[...], rows[:, b * MB : (b + 1) * MB])
+        total.part[b, :128, :] = both[:, :128]
+        total.part[b, 128:, :] = both[:, 128:]
+
+    points_rows[NC + NV :, :] = jnp.zeros((128 - NV, MB), BF16)
     for b in range(NB):
-        for j in range(MB // 128):
-            row = points[b * (MB // 128) + j : b * (MB // 128) + j + 1, :]
-            for t in range(NGRID // 128):
-                ids = lax.broadcasted_iota(jnp.int32, (128, 128), 0) + t * 128
-                grid_hot[t * 128 : (t + 1) * 128, j * 128 : (j + 1) * 128] = jnp.where(
-                    ids == row, 1.0, 0.0
-                ).astype(BF16)
-        points_rows[...] = dot(orb[...], grid_hot[...]).astype(BF16)
+        points_rows[: NC + NV, :] = dot(orb[...], grid_hot[b % 2]).astype(BF16)
 
         def make_rows(j, carry):
-            cols = pl.ds(pl.multiple_of(j * PC, PC), PC)
-            con_part = dot_tn(points_rows[:NC, :], con_hot[:, cols])
-            val_part = dot_tn(points_rows[NC:, :], val_hot[:, cols])
-            rows[b * MB : (b + 1) * MB, cols] = (con_part * val_part).astype(BF16)
+            chunk = pl.ds(pl.multiple_of(j * PC, PC), PC)
+            con_part = dot(con_hot[chunk, :], points_rows[:NC, :])
+            val_part = dot(val_hot[chunk, :], points_rows[NC:, :])
+            rows[chunk, b * MB : (b + 1) * MB] = (con_part * val_part).astype(BF16)
+            if b == 0:
+                turned[:, chunk] = trial[chunk, :].astype(F32).T.astype(BF16)
+            if b + 1 < NB:
+                for t in range(NGRID // 128 // NPC):
+                    build_grid(b + 1, j * (NGRID // 128 // NPC) + t)
             return carry
 
         lax.fori_loop(0, NPC, make_rows, 0)
-        if b == 0:
-            trial_load.wait()
-        part1[b] = dot(rows[b * MB : (b + 1) * MB, :], trial[...])
+        project(sum1, b)
         if b == 0:
             pl.semaphore_wait(barrier, 23)
         sum1.to_core(b)
@@ -216,16 +240,17 @@
             sum1.to_gather(b - 3)
 
     sum1.to_plane(NB - 1)
-
+    con_energy_load.wait()
+    val_energy_load.wait()
     con_col = jnp.broadcast_to(con_energy[...], (128, NC)).T
     val_col = jnp.broadcast_to(val_energy[...], (128, NV)).T
     con_pair = jnp.concatenate(halves(con_col), axis=1)
     val_pair = jnp.concatenate(halves(-val_col), axis=1)
 
     def make_shifted(j, carry):
-        cols = pl.ds(pl.multiple_of(j * PC, PC), PC)
-        both = dot_tn(con_hot[:, cols], con_pair) + dot_tn(val_hot[:, cols], val_pair)
-        shifted[cols, :] = (both[:, :NVEC] + both[:, NVEC:]) - filter_center
+        chunk = pl.ds(pl.multiple_of(j * PC, PC), PC)
+        both = dot(con_hot[chunk, :], con_pair) + dot(val_hot[chunk, :NV], val_pair)
+        shifted[chunk, :] = (both[:, :NVEC] + both[:, NVEC:]) - filter_center
         return carry
 
     lax.fori_loop(0, NPC, make_shifted, 0)
@@ -242,31 +267,36 @@
     def mixed_of(total):
         for b in range(NB):
             total.done(b)
-            high, low = halves(total.whole[b].reshape(MB, NVEC))
-            mixed_pair[b * MB : (b + 1) * MB, :NVEC] = high
-            mixed_pair[b * MB : (b + 1) * MB, NVEC:] = low
+            for h in range(2):
+                at = b * MB + h * 128
+                piece = total.whole[b, h * 16 : (h + 1) * 16].reshape(NVEC, 128).T
+                high, low = halves(piece)
+                mixed_pair[at : at + 128, :NVEC] = high
+                mixed_pair[at : at + 128, NVEC:] = low
         both = dot(mix[...], mixed_pair[...])
         high, low = halves(both[:, :NVEC] + both[:, NVEC:])
         mixed_pair[:, :NVEC] = high
         mixed_pair[:, NVEC:] = low
 
-    def expand(cols):
-        both = dot_tn(rows[:, cols], mixed_pair[...])
+    def expand(chunk):
+        both = dot(rows[chunk, :], mixed_pair[...])
         return both[:, :NVEC] + both[:, NVEC:]
 
     drain(sum1, NB - 2, NB - 3)
     mixed_of(sum1)
 
     def first_step(j, carry):
-        cols = pl.ds(pl.multiple_of(j * PC, PC), PC)
-        value = shifted[cols, :] * trial[cols, :].astype(F32) + expand(cols)
-        first_out[cols, :] = (value * (1.0 / filter_half)).astype(BF16)
+        chunk = pl.ds(pl.multiple_of(j * PC, PC), PC)
+        value = shifted[chunk, :] * trial[chunk, :].astype(F32) + expand(chunk)
+        rounded = (value * (1.0 / filter_half)).astype(BF16)
+        first_out[chunk, :] = rounded
+        turned[:, chunk] = rounded.astype(F32).T.astype(BF16)
         return carry
 
     lax.fori_loop(0, NPC, first_step, 0)
 
     for b in range(NB):
-        part2[b] = dot(rows[b * MB : (b + 1) * MB, :], first_out[...])
+        project(sum2, b)
         sum2.to_core(b)
         if b >= 1:
             sum2.to_plane(b - 1)
@@ -275,21 +305,32 @@
     mixed_of(sum2)
 
     def second_step(j, carry):
-        cols = pl.ds(pl.multiple_of(j * PC, PC), PC)
-        value = shifted[cols, :] * first_out[cols, :].astype(F32) + expand(cols)
-        filtered_out[cols, :] = value * (2.0 / filter_half) - trial[cols, :].astype(F32)
+        chunk = pl.ds(pl.multiple_of(j * PC, PC), PC)
+        value = shifted[chunk, :] * first_out[chunk, :].astype(F32) + expand(chunk)
+        filtered_out[chunk, :] = value * (2.0 / filter_half) - trial[chunk, :].astype(F32)
         return carry
 
     lax.fori_loop(0, NPC, second_step, 0)
     sum1.close()
     sum2.close()
+
+
+def store_kernel(first_in, filtered_in, first_out, filtered_out, sem):
+    copies = [
+        pltpu.make_async_copy(first_in, first_out, sem.at[0]),
+        pltpu.make_async_copy(filtered_in, filtered_out, sem.at[1]),
+    ]
+    for copy in copies:
+        copy.start()
+    for copy in copies:
+        copy.wait()
 
 
 def shards(
     val_orb, con_orb, val_energy, con_energy, points, val_band, con_band, kernel, trial_vecs
 ):
     vmem = pl.BlockSpec(memory_space=pltpu.VMEM)
-    away = pl.BlockSpec(memory_space=pl.ANY)
+    away = pl.BlockSpec(memory_space=pltpu.HBM)
 
     def sum_buffers():
         return [
@@ -301,22 +342,29 @@
             pltpu.VMEM((NB, 32, 8, NVEC), F32),
         ]
 
-    return pl.pallas_call(
+    shapes = (
+        jax.ShapeDtypeStruct((PAIRS, NVEC), BF16),
+        jax.ShapeDtypeStruct((PAIRS, NVEC), F32),
+    )
+    first, filtered = pl.pallas_call(
         filter_kernel,
-        out_shape=(
-            jax.ShapeDtypeStruct((PAIRS, NVEC), BF16),
-            jax.ShapeDtypeStruct((PAIRS, NVEC), F32),
-        ),
-        in_specs=[away, away, vmem, vmem, vmem, vmem, vmem, away, away],
+        out_shape=shapes,
+        in_specs=[away] * 9,
         out_specs=(vmem, vmem),
         scratch_shapes=[
+            pltpu.VMEM((1, NV), F32),
+            pltpu.VMEM((1, NC), F32),
+            pltpu.VMEM((8, 128), jnp.int32),
+            pltpu.VMEM((PAIRS // 128, 128), jnp.int32),
+            pltpu.VMEM((PAIRS // 128, 128), jnp.int32),
             pltpu.VMEM((NC + NV, NGRID), BF16),
-            pltpu.VMEM((NC, PAIRS), BF16),
-            pltpu.VMEM((NV, PAIRS), BF16),
-            pltpu.VMEM((NGRID, MB), BF16),
-            pltpu.VMEM((NC + NV, MB), BF16),
-            pltpu.VMEM((NMU, PAIRS), BF16),
+            pltpu.VMEM((PAIRS, NC), BF16),
+            pltpu.VMEM((PAIRS, 128), BF16),
+            pltpu.VMEM((2, NGRID, MB), BF16),
+            pltpu.VMEM((NC + 128, MB), BF16),
+            pltpu.VMEM((PAIRS, NMU), BF16),
             pltpu.VMEM((PAIRS, NVEC), BF16),
+            pltpu.VMEM((NVEC, PAIRS), BF16),
             pltpu.VMEM((NMU, NMU), BF16),
             pltpu.VMEM((PAIRS, NVEC), F32),
             pltpu.VMEM((NMU, 2 * NVEC), BF16),
@@ -324,7 +372,7 @@
         + sum_buffers()
         + sum_buffers()
         + [
-            pltpu.SemaphoreType.DMA((4,)),
+            pltpu.SemaphoreType.DMA((9,)),
             pltpu.SemaphoreType.DMA((5,)),
             pltpu.SemaphoreType.DMA((5, NB)),
             pltpu.SemaphoreType.DMA((5,)),
@@ -334,16 +382,29 @@
             collective_id=0, has_side_effects=True, vmem_limit_bytes=48 * 1024 * 1024
         ),
     )(
-        val_orb,
-        con_orb,
-        val_energy.reshape(1, NV),
-        con_energy.reshape(1, NC),
-        points.reshape(8, 128),
-        val_band.reshape(PAIRS // 128, 128),
-        con_band.reshape(PAIRS // 128, 128),
-        kernel,
-        trial_vecs,
+        *(
+            pltpu.with_memory_space_constraint(value, pltpu.HBM)
+            for value in (
+                val_orb,
+                con_orb,
+                val_energy.reshape(1, NV),
+                con_energy.reshape(1, NC),
+                points.reshape(8, 128),
+                val_band.reshape(PAIRS // 128, 128),
+                con_band.reshape(PAIRS // 128, 128),
+                kernel,
+                trial_vecs,
+            )
+        )
     )
+    return pl.pallas_call(
+        store_kernel,
+        out_shape=shapes,
+        in_specs=[vmem, vmem],
+        out_specs=(away, away),
+        scratch_shapes=[pltpu.SemaphoreType.DMA((2,))],
+        compiler_params=pltpu.CompilerParams(vmem_limit_bytes=1024 * 1024),
+    )(first, filtered)
 
 
 def solution(mesh):

time: 82 us -> 77.3 us (0.943)
  local copies, waits for them, and re-layouts: 7.91 us -> 0 us
  Pallas kernels: 73.1 us -> 76.6 us
    unnamed x16 -> x0, local copies, waits for them, and re-layouts: 7.91 us -> none
    pallas_call x1 -> x2, Pallas kernels: 73.1 us -> 76.6 us  [the longest x1 74.9 us: shards(): pl.pallas_call(filter_kernel, out_shape=shapes, in_specs=[away] * 9, out_...]
where the time goes in v2:
time: 77.3 us; the launch traced here: 77.2 us
  Pallas kernels  76.6 us (99%)
    pallas_call x1, Pallas kernels, shards(): pl.pallas_call(filter_kernel, out_shape=shapes, in_specs=[away] * 9, out_...  74.9 us
    pallas_call x1, Pallas kernels, shards(): pl.pallas_call(store_kernel, out_shape=shapes, in_specs=[vmem, vmem], out...  1.68 us

profile of v2, /device:TPU:1, one launch (start us, length us, event | category | flops | bytes accessed | tf_op | source)
XLA Modules:
  0.0 77.2 jit_solution(1043938625513926753)
XLA Ops:
  0.6 74.9 %shard_map.104 = (bf16[4096,128]{1,0:T(8,128)(2,1)S(1)}, f32[4096,128]{1,0:T(8,128)S(1)}) custom-call(bf16[64,2048]{1,0:T(8,128)(2,1)} %val_hbm.1, bf16[512,2048]{1,0:T(8,128)(2,1)} %con_hbm.1, f32[1,64]{1,0:T(1,128)} %bitcast.9, f32[1,512]{1,0:T(1,128)} %bitcast.8, s32[8,128]{1,0:T(8,128)} %bitcast.7, s32[32,128]{1,0:T(8,128)} %bitcast.5, ...), custom_call_target="tpu_custom_call" | custom-call | tf_op jit(solution)/shard_map/pallas_call | solution.py:349
  75.5 1.7 %shard_map.105 = (bf16[4096,128]{1,0:T(8,128)(2,1)}, f32[4096,128]{1,0:T(8,128)}) custom-call(bf16[4096,128]{1,0:T(8,128)(2,1)S(1)} %get-tuple-element.4.first_in, f32[4096,128]{1,0:T(8,128)S(1)} %get-tuple-element.5.filtered_in), custom_call_target="tpu_custom_call" | custom-call | tf_op jit(solution)/shard_map/pallas_call | solution.py:400

commit v3 on v2

--- a/solution.py
+++ b/solution.py
@@ -16,8 +16,12 @@
 PAIRS = 4096
 NB = 4
 MB = NMU // NB
+NCB = 2
+CB = NMU // NCB
 PC = 512
 NPC = PAIRS // PC
+PR = 512
+NPR = PAIRS // PR
 
 CORE, PLANE, DEPTH, GATHER, JOIN = range(5)
 PLANE_STEPS = sorted(
@@ -147,7 +151,7 @@
     kernel_hbm, trial_hbm,
     first_out, filtered_out,
     val_energy, con_energy, points, val_band, con_band,
-    orb, con_hot, val_hot, grid_hot, points_rows, rows, trial, turned, mix, shifted, mixed_pair,
+    orb, con_hot, val_hot, grid_hot, points_rows, rows, trial, turned, gathered, mix, shifted, mixed_pair,
     part1, core1, half1, plane1, depth1, whole1,
     part2, core2, half2, plane2, depth2, whole2,
     load_sem, send1, recv1, send2, recv2,
@@ -174,9 +178,9 @@
 
     def build_grid(b, t):
         ids = lax.broadcasted_iota(jnp.int32, (128, 128), 0) + t * 128
-        for j in range(MB // 128):
-            k = b * (MB // 128) + j
-            grid_hot[b % 2, pl.ds(pl.multiple_of(t * 128, 128), 128), j * 128 : (j + 1) * 128] = jnp.where(
+        for j in range(CB // 128):
+            k = b * (CB // 128) + j
+            grid_hot[b, pl.ds(pl.multiple_of(t * 128, 128), 128), j * 128 : (j + 1) * 128] = jnp.where(
                 ids == points[k : k + 1, :], 1.0, 0.0
             ).astype(BF16)
 
@@ -186,7 +190,7 @@
     con_band_load.wait()
     val_band_load.wait()
 
-    def build_hot(j, carry):
+    def build_hot(j):
         both = (con_band[pl.ds(j, 1), :] * NV + val_band[pl.ds(j, 1), :]).astype(F32)
         column = jnp.broadcast_to(both, (128, 128)).T.astype(jnp.int32)
         con_column = lax.shift_right_logical(column, 6)
@@ -196,9 +200,13 @@
         for t in range(NC // 128):
             con_hot[pairs, t * 128 : (t + 1) * 128] = jnp.where(ids + t * 128 == con_column, 1.0, 0.0).astype(BF16)
         val_hot[pairs, :] = jnp.where(ids == val_column, 1.0, 0.0).astype(BF16)
+
+    def build_four(j, carry):
+        for k in range(4):
+            build_hot(4 * j + k)
         return carry
 
-    lax.fori_loop(0, PAIRS // 128, build_hot, 0)
+    lax.fori_loop(0, PAIRS // 512, build_four, 0)
     con_load.wait()
     val_load.wait()
     trial_load.wait()
@@ -206,40 +214,49 @@
     sum1 = Sum(place, part1, core1, half1, plane1, depth1, whole1, send1, recv1)
     sum2 = Sum(place, part2, core2, half2, plane2, depth2, whole2, send2, recv2)
 
-    def project(total, b):
-        both = dot(turned[...], rows[:, b * MB : (b + 1) * MB])
-        total.part[b, :128, :] = both[:, :128]
-        total.part[b, 128:, :] = both[:, 128:]
-
-    points_rows[NC + NV :, :] = jnp.zeros((128 - NV, MB), BF16)
-    for b in range(NB):
-        points_rows[: NC + NV, :] = dot(orb[...], grid_hot[b % 2]).astype(BF16)
+    def project(chunk, lanes):
+        return dot(turned[:, chunk], rows[chunk, lanes])
+
+    def keep(total, first, value):
+        for k in range(value.shape[1] // 128):
+            b, h = first + k // 2, k % 2
+            total.part[b, h * 128 : (h + 1) * 128, :] = value[:, k * 128 : (k + 1) * 128]
+
+    points_rows[NC + NV :, :] = jnp.zeros((128 - NV, CB), BF16)
+    for c in range(NCB):
+        points_rows[: NC + NV, :] = dot(orb[...], grid_hot[c]).astype(BF16)
+        if c == 0:
+            for t in range(NGRID // 128):
+                build_grid(1, t)
+            for k in range(NPC):
+                chunk = slice(k * PC, (k + 1) * PC)
+                turned[:, chunk] = trial[chunk, :].astype(F32).T.astype(BF16)
+        if c == 1:
+            for b in range(NB // 2):
+                sum1.to_plane(b)
+        block = slice(c * CB, (c + 1) * CB)
 
         def make_rows(j, carry):
-            chunk = pl.ds(pl.multiple_of(j * PC, PC), PC)
+            chunk = pl.ds(pl.multiple_of(j * PR, PR), PR)
+            before = pl.ds(pl.multiple_of(jnp.maximum(j - 1, 0) * PR, PR), PR)
+            so_far = gathered[:, :CB] + project(before, block)
+            gathered[:, :CB] = jnp.where(j > 0, so_far, 0.0)
             con_part = dot(con_hot[chunk, :], points_rows[:NC, :])
             val_part = dot(val_hot[chunk, :], points_rows[NC:, :])
-            rows[chunk, b * MB : (b + 1) * MB] = (con_part * val_part).astype(BF16)
-            if b == 0:
-                turned[:, chunk] = trial[chunk, :].astype(F32).T.astype(BF16)
-            if b + 1 < NB:
-                for t in range(NGRID // 128 // NPC):
-                    build_grid(b + 1, j * (NGRID // 128 // NPC) + t)
+            rows[chunk, block] = (con_part * val_part).astype(BF16)
             return carry
 
-        lax.fori_loop(0, NPC, make_rows, 0)
-        project(sum1, b)
-        if b == 0:
+        lax.fori_loop(0, NPR, make_rows, 0)
+        keep(sum1, c * 2, gathered[:, :CB] + project(slice(PAIRS - PR, PAIRS), block))
+        if c == 0:
             pl.semaphore_wait(barrier, 23)
-        sum1.to_core(b)
-        if b >= 1:
-            sum1.to_plane(b - 1)
-        if b >= 2:
-            sum1.to_depth(b - 2)
-        if b >= 3:
-            sum1.to_gather(b - 3)
-
-    sum1.to_plane(NB - 1)
+        sum1.to_core(c * 2)
+        sum1.to_core(c * 2 + 1)
+
+    for b in range(NB // 2):
+        sum1.to_depth(b)
+    for b in range(NB // 2, NB):
+        sum1.to_plane(b)
     con_energy_load.wait()
     val_energy_load.wait()
     con_col = jnp.broadcast_to(con_energy[...], (128, NC)).T
@@ -255,14 +272,6 @@
 
     lax.fori_loop(0, NPC, make_shifted, 0)
     mix_load.wait()
-
-    def drain(total, plane_from, gather_from):
-        for b in range(plane_from, NB):
-            total.to_depth(b)
-        for b in range(gather_from, NB):
-            total.to_gather(b)
-        for b in range(NB):
-            total.to_join(b)
 
     def mixed_of(total):
         for b in range(NB):
@@ -282,11 +291,21 @@
         both = dot(rows[chunk, :], mixed_pair[...])
         return both[:, :NVEC] + both[:, NVEC:]
 
-    drain(sum1, NB - 2, NB - 3)
+    for b in range(NB // 2):
+        sum1.to_gather(b)
+    for b in range(NB // 2, NB):
+        sum1.to_depth(b)
+    for b in range(NB // 2, NB):
+        sum1.to_gather(b)
+    for b in range(NB):
+        sum1.to_join(b)
     mixed_of(sum1)
 
     def first_step(j, carry):
         chunk = pl.ds(pl.multiple_of(j * PC, PC), PC)
+        before = pl.ds(pl.multiple_of(jnp.maximum(j - 1, 0) * PC, PC), PC)
+        so_far = gathered[...] + project(before, slice(None))
+        gathered[...] = jnp.where(j > 0, so_far, 0.0)
         value = shifted[chunk, :] * trial[chunk, :].astype(F32) + expand(chunk)
         rounded = (value * (1.0 / filter_half)).astype(BF16)
         first_out[chunk, :] = rounded
@@ -294,14 +313,17 @@
         return carry
 
     lax.fori_loop(0, NPC, first_step, 0)
-
-    for b in range(NB):
-        project(sum2, b)
+    keep(sum2, 0, gathered[...] + project(slice(PAIRS - PC, PAIRS), slice(None)))
+    for b in range(NB):
         sum2.to_core(b)
-        if b >= 1:
-            sum2.to_plane(b - 1)
-    sum2.to_plane(NB - 1)
-    drain(sum2, 0, 0)
+    for b in range(NB):
+        sum2.to_plane(b)
+    for b in range(NB):
+        sum2.to_depth(b)
+    for b in range(NB):
+        sum2.to_gather(b)
+    for b in range(NB):
+        sum2.to_join(b)
     mixed_of(sum2)
 
     def second_step(j, carry):
@@ -360,11 +382,12 @@
             pltpu.VMEM((NC + NV, NGRID), BF16),
             pltpu.VMEM((PAIRS, NC), BF16),
             pltpu.VMEM((PAIRS, 128), BF16),
-            pltpu.VMEM((2, NGRID, MB), BF16),
-            pltpu.VMEM((NC + 128, MB), BF16),
+            pltpu.VMEM((NCB, NGRID, CB), BF16),
+            pltpu.VMEM((NC + 128, CB), BF16),
             pltpu.VMEM((PAIRS, NMU), BF16),
             pltpu.VMEM((PAIRS, NVEC), BF16),
             pltpu.VMEM((NVEC, PAIRS), BF16),
+            pltpu.VMEM((NVEC, NMU), F32),
             pltpu.VMEM((NMU, NMU), BF16),
             pltpu.VMEM((PAIRS, NVEC), F32),
             pltpu.VMEM((NMU, 2 * NVEC), BF16),

time: 77.3 us -> 72.3 us (0.935)
  Pallas kernels: 76.6 us -> 71.5 us
    pallas_call x1, Pallas kernels: 74.9 us -> 69.9 us  [shards(): pl.pallas_call(filter_kernel, out_shape=shapes, in_specs=[away] * 9, out_...]
where the time goes in v3:
time: 72.3 us; the launch traced here: 72.2 us
  Pallas kernels  71.5 us (99%)
    pallas_call x1, Pallas kernels, shards(): pl.pallas_call(filter_kernel, out_shape=shapes, in_specs=[away] * 9, out_...  69.9 us
    pallas_call x1, Pallas kernels, shards(): pl.pallas_call(store_kernel, out_shape=shapes, in_specs=[vmem, vmem], out...  1.68 us

profile of v3, /device:TPU:1, one launch (start us, length us, event | category | flops | bytes accessed | tf_op | source)
XLA Modules:
  0.0 72.2 jit_solution(6405123306605459619)
XLA Ops:
  0.6 69.9 %shard_map.104 = (bf16[4096,128]{1,0:T(8,128)(2,1)S(1)}, f32[4096,128]{1,0:T(8,128)S(1)}) custom-call(bf16[64,2048]{1,0:T(8,128)(2,1)} %val_hbm.1, bf16[512,2048]{1,0:T(8,128)(2,1)} %con_hbm.1, f32[1,64]{1,0:T(1,128)} %bitcast.9, f32[1,512]{1,0:T(1,128)} %bitcast.8, s32[8,128]{1,0:T(8,128)} %bitcast.7, s32[32,128]{1,0:T(8,128)} %bitcast.5, ...), custom_call_target="tpu_custom_call" | custom-call | tf_op jit(solution)/shard_map/pallas_call | solution.py:371
  70.5 1.7 %shard_map.105 = (bf16[4096,128]{1,0:T(8,128)(2,1)}, f32[4096,128]{1,0:T(8,128)}) custom-call(bf16[4096,128]{1,0:T(8,128)(2,1)S(1)} %get-tuple-element.4.first_in, f32[4096,128]{1,0:T(8,128)S(1)} %get-tuple-element.5.filtered_in), custom_call_target="tpu_custom_call" | custom-call | tf_op jit(solution)/shard_map/pallas_call | solution.py:423

commit v4 on v3

--- a/solution.py
+++ b/solution.py
@@ -18,9 +18,12 @@
 MB = NMU // NB
 NCB = 2
 CB = NMU // NCB
-PC = 512
-NPC = PAIRS // PC
-PR = 512
+PF = 1024
+NPF = PAIRS // PF
+PL = 1024
+NPL = PAIRS // PL
+PE = 1024
+PR = 1024
 NPR = PAIRS // PR
 
 CORE, PLANE, DEPTH, GATHER, JOIN = range(5)
@@ -149,9 +152,9 @@
 def filter_kernel(
     val_hbm, con_hbm, val_energy_hbm, con_energy_hbm, points_hbm, val_band_hbm, con_band_hbm,
     kernel_hbm, trial_hbm,
-    first_out, filtered_out,
+    first_out, rows, trial, shifted, mixed_pair,
     val_energy, con_energy, points, val_band, con_band,
-    orb, con_hot, val_hot, grid_hot, points_rows, rows, trial, turned, gathered, mix, shifted, mixed_pair,
+    orb, con_hot, val_hot, grid_hot, points_rows, turned, gathered, mix,
     part1, core1, half1, plane1, depth1, whole1,
     part2, core2, half2, plane2, depth2, whole2,
     load_sem, send1, recv1, send2, recv2,
@@ -184,9 +187,13 @@
                 ids == points[k : k + 1, :], 1.0, 0.0
             ).astype(BF16)
 
+    def build_first_grid(t, carry):
+        build_grid(0, t)
+        build_grid(1, t)
+        return carry
+
     points_load.wait()
-    for t in range(NGRID // 128):
-        build_grid(0, t)
+    lax.fori_loop(0, NGRID // 128, build_first_grid, 0)
     con_band_load.wait()
     val_band_load.wait()
 
@@ -201,15 +208,8 @@
             con_hot[pairs, t * 128 : (t + 1) * 128] = jnp.where(ids + t * 128 == con_column, 1.0, 0.0).astype(BF16)
         val_hot[pairs, :] = jnp.where(ids == val_column, 1.0, 0.0).astype(BF16)
 
-    def build_four(j, carry):
-        for k in range(4):
-            build_hot(4 * j + k)
-        return carry
-
-    lax.fori_loop(0, PAIRS // 512, build_four, 0)
     con_load.wait()
     val_load.wait()
-    trial_load.wait()
 
     sum1 = Sum(place, part1, core1, half1, plane1, depth1, whole1, send1, recv1)
     sum2 = Sum(place, part2, core2, half2, plane2, depth2, whole2, send2, recv2)
@@ -224,13 +224,20 @@
 
     points_rows[NC + NV :, :] = jnp.zeros((128 - NV, CB), BF16)
     for c in range(NCB):
-        points_rows[: NC + NV, :] = dot(orb[...], grid_hot[c]).astype(BF16)
+        steps = 4 if c == 0 else 2
+        height = (NC + NV) // steps
+
+        def pick_points(j, carry):
+            some = pl.ds(pl.multiple_of(j * height, height), height)
+            points_rows[some, :] = dot(orb[some, :], grid_hot[c]).astype(BF16)
+            if c == 0:
+                for k in range(PAIRS // 128 // steps):
+                    build_hot(j * (PAIRS // 128 // steps) + k)
+            return carry
+
+        lax.fori_loop(0, steps, pick_points, 0)
         if c == 0:
-            for t in range(NGRID // 128):
-                build_grid(1, t)
-            for k in range(NPC):
-                chunk = slice(k * PC, (k + 1) * PC)
-                turned[:, chunk] = trial[chunk, :].astype(F32).T.astype(BF16)
+            trial_load.wait()
         if c == 1:
             for b in range(NB // 2):
                 sum1.to_plane(b)
@@ -244,6 +251,8 @@
             con_part = dot(con_hot[chunk, :], points_rows[:NC, :])
             val_part = dot(val_hot[chunk, :], points_rows[NC:, :])
             rows[chunk, block] = (con_part * val_part).astype(BF16)
+            if c == 0:
+                turned[:, chunk] = trial[chunk, :].astype(F32).T.astype(BF16)
             return carry
 
         lax.fori_loop(0, NPR, make_rows, 0)
@@ -265,12 +274,12 @@
     val_pair = jnp.concatenate(halves(-val_col), axis=1)
 
     def make_shifted(j, carry):
-        chunk = pl.ds(pl.multiple_of(j * PC, PC), PC)
+        chunk = pl.ds(pl.multiple_of(j * PE, PE), PE)
         both = dot(con_hot[chunk, :], con_pair) + dot(val_hot[chunk, :NV], val_pair)
         shifted[chunk, :] = (both[:, :NVEC] + both[:, NVEC:]) - filter_center
         return carry
 
-    lax.fori_loop(0, NPC, make_shifted, 0)
+    lax.fori_loop(0, PAIRS // PE, make_shifted, 0)
     mix_load.wait()
 
     def mixed_of(total):
@@ -302,8 +311,8 @@
     mixed_of(sum1)
 
     def first_step(j, carry):
-        chunk = pl.ds(pl.multiple_of(j * PC, PC), PC)
-        before = pl.ds(pl.multiple_of(jnp.maximum(j - 1, 0) * PC, PC), PC)
+        chunk = pl.ds(pl.multiple_of(j * PF, PF), PF)
+        before = pl.ds(pl.multiple_of(jnp.maximum(j - 1, 0) * PF, PF), PF)
         so_far = gathered[...] + project(before, slice(None))
         gathered[...] = jnp.where(j > 0, so_far, 0.0)
         value = shifted[chunk, :] * trial[chunk, :].astype(F32) + expand(chunk)
@@ -312,8 +321,8 @@
         turned[:, chunk] = rounded.astype(F32).T.astype(BF16)
         return carry
 
-    lax.fori_loop(0, NPC, first_step, 0)
-    keep(sum2, 0, gathered[...] + project(slice(PAIRS - PC, PAIRS), slice(None)))
+    lax.fori_loop(0, NPF, first_step, 0)
+    keep(sum2, 0, gathered[...] + project(slice(PAIRS - PF, PAIRS), slice(None)))
     for b in range(NB):
         sum2.to_core(b)
     for b in range(NB):
@@ -326,26 +335,29 @@
         sum2.to_join(b)
     mixed_of(sum2)
 
-    def second_step(j, carry):
-        chunk = pl.ds(pl.multiple_of(j * PC, PC), PC)
-        value = shifted[chunk, :] * first_out[chunk, :].astype(F32) + expand(chunk)
-        filtered_out[chunk, :] = value * (2.0 / filter_half) - trial[chunk, :].astype(F32)
-        return carry
-
-    lax.fori_loop(0, NPC, second_step, 0)
     sum1.close()
     sum2.close()
 
 
-def store_kernel(first_in, filtered_in, first_out, filtered_out, sem):
-    copies = [
-        pltpu.make_async_copy(first_in, first_out, sem.at[0]),
-        pltpu.make_async_copy(filtered_in, filtered_out, sem.at[1]),
-    ]
-    for copy in copies:
-        copy.start()
-    for copy in copies:
-        copy.wait()
+def last_kernel(first_in, rows, trial, shifted, mixed_pair, first_out, filtered_out, filtered, sem):
+    first_copy = pltpu.make_async_copy(first_in, first_out, sem.at[NPL])
+    first_copy.start()
+
+    def store(j, chunk):
+        return pltpu.make_async_copy(filtered.at[chunk], filtered_out.at[chunk], sem.at[j])
+
+    def second_step(j, carry):
+        chunk = pl.ds(pl.multiple_of(j * PL, PL), PL)
+        both = dot(rows[chunk, :], mixed_pair[...])
+        value = shifted[chunk, :] * first_in[chunk, :].astype(F32) + (both[:, :NVEC] + both[:, NVEC:])
+        filtered[chunk, :] = value * (2.0 / filter_half) - trial[chunk, :].astype(F32)
+        store(j, chunk).start()
+        return carry
+
+    lax.fori_loop(0, NPL, second_step, 0)
+    for j in range(NPL):
+        store(j, slice(j * PL, (j + 1) * PL)).wait()
+    first_copy.wait()
 
 
 def shards(
@@ -368,11 +380,17 @@
         jax.ShapeDtypeStruct((PAIRS, NVEC), BF16),
         jax.ShapeDtypeStruct((PAIRS, NVEC), F32),
     )
-    first, filtered = pl.pallas_call(
+    kept = pl.pallas_call(
         filter_kernel,
-        out_shape=shapes,
+        out_shape=(
+            jax.ShapeDtypeStruct((PAIRS, NVEC), BF16),
+            jax.ShapeDtypeStruct((PAIRS, NMU), BF16),
+            jax.ShapeDtypeStruct((PAIRS, NVEC), BF16),
+            jax.ShapeDtypeStruct((PAIRS, NVEC), F32),
+            jax.ShapeDtypeStruct((NMU, 2 * NVEC), BF16),
+        ),
         in_specs=[away] * 9,
-        out_specs=(vmem, vmem),
+        out_specs=(vmem,) * 5,
         scratch_shapes=[
             pltpu.VMEM((1, NV), F32),
             pltpu.VMEM((1, NC), F32),
@@ -384,13 +402,9 @@
             pltpu.VMEM((PAIRS, 128), BF16),
             pltpu.VMEM((NCB, NGRID, CB), BF16),
             pltpu.VMEM((NC + 128, CB), BF16),
-            pltpu.VMEM((PAIRS, NMU), BF16),
-            pltpu.VMEM((PAIRS, NVEC), BF16),
             pltpu.VMEM((NVEC, PAIRS), BF16),
             pltpu.VMEM((NVEC, NMU), F32),
             pltpu.VMEM((NMU, NMU), BF16),
-            pltpu.VMEM((PAIRS, NVEC), F32),
-            pltpu.VMEM((NMU, 2 * NVEC), BF16),
         ]
         + sum_buffers()
         + sum_buffers()
@@ -402,7 +416,7 @@
             pltpu.SemaphoreType.DMA((5, NB)),
         ],
         compiler_params=pltpu.CompilerParams(
-            collective_id=0, has_side_effects=True, vmem_limit_bytes=48 * 1024 * 1024
+            collective_id=0, has_side_effects=True, vmem_limit_bytes=36 * 1024 * 1024
         ),
     )(
         *(
@@ -421,13 +435,13 @@
         )
     )
     return pl.pallas_call(
-        store_kernel,
+        last_kernel,
         out_shape=shapes,
-        in_specs=[vmem, vmem],
+        in_specs=[vmem] * 5,
         out_specs=(away, away),
-        scratch_shapes=[pltpu.SemaphoreType.DMA((2,))],
-        compiler_params=pltpu.CompilerParams(vmem_limit_bytes=1024 * 1024),
-    )(first, filtered)
+        scratch_shapes=[pltpu.VMEM((PAIRS, NVEC), F32), pltpu.SemaphoreType.DMA((NPL + 1,))],
+        compiler_params=pltpu.CompilerParams(vmem_limit_bytes=8 * 1024 * 1024),
+    )(*kept)
 
 
 def solution(mesh):

time: 72.3 us -> 67.8 us (0.938)
  Pallas kernels: 71.5 us -> 67 us
    pallas_call x2, Pallas kernels: 71.5 us -> 67 us  [the longest x1 63.3 us: shards(): pl.pallas_call(filter_kernel, out_shape=(jax.ShapeDtypeStruct((PAIRS, NVE...]
where the time goes in v4:
time: 67.8 us; the launch traced here: 67.6 us
  Pallas kernels  67 us (99%)
    pallas_call x1, Pallas kernels, shards(): pl.pallas_call(filter_kernel, out_shape=(jax.ShapeDtypeStruct((PAIRS, NVE...  63.3 us
    pallas_call x1, Pallas kernels, shards(): pl.pallas_call(last_kernel, out_shape=shapes, in_specs=[vmem] * 5, out_sp...  3.69 us

profile of v4, /device:TPU:1, one launch (start us, length us, event | category | flops | bytes accessed | tf_op | source)
XLA Modules:
  0.0 67.6 jit_solution(2919162817604835473)
XLA Ops:
  0.6 63.3 %shard_map.104 = (bf16[4096,128]{1,0:T(8,128)(2,1)S(1)}, bf16[4096,1024]{1,0:T(8,128)(2,1)S(1)}, bf16[4096,128]{1,0:T(8,128)(2,1)S(1)}, f32[4096,128]{1,0:T(8,128)S(1)}, bf16[1024,256]{1,0:T(8,128)(2,1)S(1)}) custom-call(bf16[64,2048]{1,0:T(8,128)(2,1)} %val_hbm.1, bf16[512,2048]{1,0:T(8,128)(2,1)} %con_hbm.1, f32[1,64]{1,0:T(1,128)} %bitcast.9, ...), custom_call_target="tpu_custom_call" | custom-call | tf_op jit(solution)/shard_map/pallas_call | solution.py:383
  63.9 3.7 %shard_map.105 = (bf16[4096,128]{1,0:T(8,128)(2,1)}, f32[4096,128]{1,0:T(8,128)}) custom-call(bf16[4096,128]{1,0:T(8,128)(2,1)S(1)} %get-tuple-element.7.first_in, bf16[4096,1024]{1,0:T(8,128)(2,1)S(1)} %get-tuple-element.8.rows, bf16[4096,128]{1,0:T(8,128)(2,1)S(1)} %get-tuple-element.9.trial, f32[4096,128]{1,0:T(8,128)S(1)} %get-tuple-element.10.shifted, ...), custom_call_target="tpu_custom_call" | custom-call | tf_op jit(solution)/shard_map/pallas_call | solution.py:437
